TPU v7x, 256 devices: a whole 4x4x8 slice. The times are simulated.
256 devices in a mesh: dp: 64 (over x, z, core), proto: 4 (over y).
Axes of the slice: x: 4, y: 4, z: 8, core: 2. Of those that a mesh axis runs over, the one named last changes fastest.
Arguments:
- embeddings: bfloat16 [65536, 1024], P(('dp', 'proto')), may hold values from -6 to 6
- centres: bfloat16 [8192, 1024], P('proto'), may hold values from -0.1875 to 0.1875
Outputs:
- updated: bfloat16 [8192, 1024], P('proto')
All inputs are finite; a program needn't handle non-finite values.
Results may differ from a plain program's by a relative error of at most 0.0074.
Values may be sent and summed in bfloat16 or wider, within the bound.
A program may use at most 64 MiB of HBM per device.

v0:
```python
import jax
import jax.numpy as jnp
from jax import lax
from jax.sharding import PartitionSpec as P

ITERS = 3


def normalise(rows):
    values = rows.astype(jnp.float32)
    scaled = values * lax.rsqrt(jnp.mean(values * values, axis=1, keepdims=True) + 1e-05)
    return scaled.astype(jnp.bfloat16)


def column_total(partial_sum):
    return lax.psum(partial_sum, "dp")


def row_total(partial_sum):
    return lax.psum(partial_sum, "proto")


def per_device(embeddings, centres):
    unit = normalise(embeddings)
    group = lax.all_gather(unit, "proto", axis=0, tiled=True)
    scores = lax.dot_general(
        group, centres, (((1,), (1,)), ((), ())), preferred_element_type=jnp.float32
    )
    plan = jnp.exp(4.0 * scores)
    total_rows = group.shape[0] * lax.axis_size("dp")
    total_cols = centres.shape[0] * lax.axis_size("proto")
    for step in range(ITERS):
        colsum = column_total(jnp.sum(plan, axis=0))
        plan = plan / (total_cols * colsum)[None, :]
        rowsum = row_total(jnp.sum(plan, axis=1))
        plan = plan / (total_rows * rowsum)[:, None]
    codes = (total_rows * plan).astype(jnp.bfloat16)
    share = lax.psum_scatter(
        lax.dot_general(codes, group, (((0,), (0,)), ((), ())), preferred_element_type=jnp.float32),
        "dp",
        scatter_dimension=0,
        tiled=True,
    )
    rescaled = share * lax.rsqrt(jnp.mean(share * share, axis=1, keepdims=True) + 1e-05)
    return lax.all_gather(rescaled.astype(jnp.bfloat16), "dp", axis=0, tiled=True)


def solution(mesh):
    return jax.shard_map(
        per_device,
        mesh=mesh,
        in_specs=(P(("dp", "proto"), None), P("proto", None)),
        out_specs=P("proto", None),
        check_vma=False,
    )
```

profile of v0, /device:TPU:1, one launch (start us, length us, event | category | flops | bytes accessed | tf_op | source)
XLA Modules:
  0.0 737.2 jit_solution(6118723697224441080)
XLA Ops:
  6.5 0.0 all-gather.3.cloned.1.call-start
  6.5 1.2 fusion.15
  7.8 2.0 fusion.16
  9.8 0.0 all-gather.3.cloned.1.call-update
  9.8 0.0 reduce-scatter.2.cloned.1.call-start
  9.8 37.1 %all-gather.3.cloned.1.call-done = bf16[1024,1024]{1,0:T(8,128)(2,1)} async-done(((bf16[256,1024]{1,0:T(8,128)(2,1)}), bf16[1024,1024]{1,0:T(8,128)(2,1)}) %all-gather.3.cloned.1.call-update) | async-done | bytes 2097168 | tf_op jit(solution)/shard_map/all_gather | solution.py:25
  46.9 10.6 %fusion.18 = (f32[2048]{0:T(1024)S(1)}, f32[1024,2048]{1,0:T(8,128)}) fusion(bf16[1024,1024]{1,0:T(8,128)(2,1)} %all-gather.3.cloned.1.call-done, bf16[2048,1024]{1,0:T(8,128)(2,1)} %param.3), kind=kOutput, calls=%fused_computation.33 | convolution fusion | flops 4299159552 | bytes 14688256 | tf_op jit(solution)/shard_map/dot_general | solution.py:26
  57.5 126.7 %psum.42 = f32[2048]{0:T(1024)S(1)} all-reduce(f32[2048]{0:T(1024)S(1)} %get-tuple-element.5), channel_id=1, replica_groups=mesh['dp'=64,'proto'=4] {'dp'}, use_global_device_ids=true, to_apply=%region_2.0 | all-reduce | flops 2048 | bytes 16384 | tf_op jit(solution)/shard_map/psum | solution.py:16
  184.3 4.0 divide_reduce_fusion
  188.3 6.6 psum.43
  194.9 4.2 fusion.8
  199.0 132.3 %psum.44 = f32[2048]{0:T(1024)S(1)} all-reduce(f32[2048]{0:T(1024)S(1)} %fusion.8), channel_id=1, replica_groups=mesh['dp'=64,'proto'=4] {'dp'}, use_global_device_ids=true, to_apply=%region_6.0 | all-reduce | flops 2048 | bytes 16384 | tf_op jit(solution)/shard_map/psum | solution.py:16
  331.4 4.4 fusion.10
  335.8 6.9 psum.45
  342.7 0.0 copy-start
  342.7 4.6 fusion.11
  347.3 128.1 %psum.46 = f32[2048]{0:T(1024)S(1)} all-reduce(f32[2048]{0:T(1024)S(1)} %fusion.11), channel_id=1, replica_groups=mesh['dp'=64,'proto'=4] {'dp'}, use_global_device_ids=true, to_apply=%region_10.0 | all-reduce | flops 2048 | bytes 16384 | tf_op jit(solution)/shard_map/psum | solution.py:16
  475.4 4.7 fusion.12
  480.1 6.6 psum.47
  486.7 0.0 copy-done
  486.7 12.4 %fusion.13 = f32[2048,1024]{1,0:T(8,128)} fusion(bf16[1024,1024]{1,0:T(8,128)(2,1)S(1)} %copy-done, f32[1024,2048]{1,0:T(8,128)} %get-tuple-element.6, f32[1024]{0:T(1024)S(1)} %broadcast_multiply_fusion.3, f32[2048]{0:T(1024)S(1)} %broadcast_multiply_fusion, f32[1024]{0:T(1024)S(1)} %broadcast_multiply_fusion.4, f32[2048]{0:T(1024)S(1)} %broadcast_multiply_fusion.1, ...), kind=kOutput, calls=%fused_computation.17 | convolution fusion | flops 4311744512 | bytes 18911232 | tf_op jit(solution)/shard_map/dot_general | solution.py:39
  499.1 0.0 reduce-scatter.2.cloned.1.call-update
  499.2 0.0 all-gather.5.cloned.1.call-start
  499.2 141.6 %reduce-scatter.2.cloned.1.call-done = f32[32,1024]{1,0:T(8,128)} async-done(((f32[2048,1024]{1,0:T(8,128)}), f32[32,1024]{1,0:T(8,128)}) %reduce-scatter.2.cloned.1.call-update) | async-done | bytes 131088 | tf_op jit(solution)/shard_map/reduce_scatter | solution.py:38
  640.8 1.0 multiply_reduce_fusion
  641.8 1.6 multiply_convert_fusion
  643.4 0.0 all-gather.5.cloned.1.call-update
  643.5 82.6 %all-gather.5.cloned.1.call-done = bf16[2048,1024]{1,0:T(8,128)(2,1)} async-done(((bf16[32,1024]{1,0:T(8,128)(2,1)}), bf16[2048,1024]{1,0:T(8,128)(2,1)}) %all-gather.5.cloned.1.call-update) | async-done | bytes 4194320 | tf_op jit(solution)/shard_map/all_gather | solution.py:45
  726.1 4.6 copy.4
  (8 shorter events, 0.0 us)
Async XLA Ops:
  6.5 40.4 %all-gather.3.cloned.1.call-start = ((), (), s32[]{:S(2)}) async-start(), calls=%async_computation.1 | async-start | bytes 2621440 | tf_op jit(solution)/shard_map/all_gather | solution.py:25
  9.8 631.0 %reduce-scatter.2.cloned.1.call-start = ((), (), s32[]{:S(2)}) async-start(), calls=%async_computation.2 | async-start | bytes 8519680 | tf_op jit(solution)/shard_map/reduce_scatter | solution.py:38
  342.7 144.0 %copy-start = (bf16[1024,1024]{1,0:T(8,128)(2,1)S(1)}, bf16[1024,1024]{1,0:T(8,128)(2,1)}, u32[]{:S(2)}) copy-start(bf16[1024,1024]{1,0:T(8,128)(2,1)} %all-gather.3.cloned.1.call-done) | copy-start | bytes 6291460
  499.2 226.9 %all-gather.5.cloned.1.call-start = ((), (), s32[]{:S(2)}) async-start(), calls=%async_computation.3 | async-start | bytes 4259840 | tf_op jit(solution)/shard_map/all_gather | solution.py:45
Sparse Core Ops, SparseCore 0:
  9.9 36.9 all-gather.2
  499.3 141.4 reduce-scatter.1
  643.6 82.4 all-gather.4
where the time goes:
time: 738 us; the launch traced here: 737 us
  blocking collectives  407 us (55%)
  waiting for transfers between devices  261 us (35%)
  other arithmetic  27.7 us (4%)
  matrix products  23.1 us (3%)
  between operations  13.2 us (2%)
    psum x3, blocking collectives, column_total(): return lax.psum(partial_sum, 'dp')  387 us
    reduce_scatter x1, waiting for transfers between devices, per_device(): lax.psum_scatter(lax.dot_general(codes, group, (((0,), (0,)), ((), ())),...  142 us
    all_gather x1, waiting for transfers between devices, per_device(): lax.all_gather(rescaled.astype(jnp.bfloat16), 'dp', axis=0, tiled=True)  82.6 us
    all_gather x1, waiting for transfers between devices, per_device(): group = lax.all_gather(unit, 'proto', axis=0, tiled=True)  37.1 us
    psum x3, blocking collectives, row_total(): return lax.psum(partial_sum, 'proto')  20 us
  transfers between devices with their start and end apart: 3, of which 3 were waited for; matrix products, arithmetic and copies ran while one was open for 0% of the time, Pallas kernels for 0%

commit v1 on v0

--- a/solution.py
+++ b/solution.py
@@ -4,6 +4,7 @@
 from jax.sharding import PartitionSpec as P
 
 ITERS = 3
+levels_all_get = lambda vec, mesh_dim: jnp.sum(lax.all_gather(vec, axis_name=mesh_dim), axis=0)
 
 
 def normalise(rows):
@@ -13,7 +14,7 @@
 
 
 def column_total(partial_sum):
-    return lax.psum(partial_sum, "dp")
+    return levels_all_get(partial_sum, "dp")
 
 
 def row_total(partial_sum):

time: 738 us -> 508 us (0.69)
  blocking collectives: 407 us -> 173 us
    psum x3 -> x0, blocking collectives: 387 us -> none  [column_total(): return lax.psum(partial_sum, 'dp')]
    all_gather x0 -> x3, blocking collectives: none -> 153 us  [lax.all_gather(vec, axis_name=mesh_dim)]
where the time goes in v1:
time: 508 us
  waiting for transfers between devices  265 us (52%)
  blocking collectives  173 us (34%)
  other arithmetic  27.9 us (5%)
  matrix products  23.1 us (5%)
  between operations  13.2 us (3%)
    all_gather x3, blocking collectives, lax.all_gather(vec, axis_name=mesh_dim)  153 us
    reduce_scatter x1, waiting for transfers between devices, per_device(): lax.psum_scatter(lax.dot_general(codes, group, (((0,), (0,)), ((), ())),...  146 us
    all_gather x1, waiting for transfers between devices, per_device(): lax.all_gather(rescaled.astype(jnp.bfloat16), 'dp', axis=0, tiled=True)  82.6 us
    all_gather x1, waiting for transfers between devices, per_device(): group = lax.all_gather(unit, 'proto', axis=0, tiled=True)  37.1 us
    psum x3, blocking collectives, row_total(): return lax.psum(partial_sum, 'proto')  20 us
    reduce_sum x3, other arithmetic, per_device(): rowsum = row_total(jnp.sum(plan, axis=1))  13 us
    dot_general x1, matrix products, per_device(): lax.dot_general(codes, group, (((0,), (0,)), ((), ())), preferred_element...  12.5 us
    dot_general x1, matrix products, per_device(): lax.dot_general(group, centres, (((1,), (1,)), ((), ())), preferred_eleme...  10.6 us
  transfers between devices with their start and end apart: 3, of which 3 were waited for; matrix products, arithmetic and copies ran while one was open for 0% of the time, Pallas kernels for 0%

profile of v1, /device:TPU:1, one launch (start us, length us, event | category | flops | bytes accessed | tf_op | source)
XLA Modules:
  0.0 508.1 jit_solution(13323348025492630326)
XLA Ops:
  6.5 0.0 all-gather.6.cloned.1.call-start
  6.5 1.2 fusion.15
  7.8 2.0 fusion.16
  9.8 0.0 all-gather.6.cloned.1.call-update
  9.8 0.0 reduce-scatter.2.cloned.1.call-start
  9.8 37.1 %all-gather.6.cloned.1.call-done = bf16[1024,1024]{1,0:T(8,128)(2,1)} async-done(((bf16[256,1024]{1,0:T(8,128)(2,1)}), bf16[1024,1024]{1,0:T(8,128)(2,1)}) %all-gather.6.cloned.1.call-update) | async-done | bytes 2097168 | tf_op jit(solution)/shard_map/all_gather | solution.py:26
  46.9 10.6 %fusion.18 = (f32[2048]{0:T(1024)S(1)}, f32[1024,2048]{1,0:T(8,128)}) fusion(bf16[1024,1024]{1,0:T(8,128)(2,1)} %all-gather.6.cloned.1.call-done, bf16[2048,1024]{1,0:T(8,128)(2,1)} %param.3), kind=kOutput, calls=%fused_computation.33 | convolution fusion | flops 4299159552 | bytes 14688256 | tf_op jit(solution)/shard_map/dot_general | solution.py:27
  57.5 51.9 %all-gather = f32[131072]{0:T(1024)S(1)} all-gather(f32[2048]{0:T(1024)S(1)} %get-tuple-element.5), channel_id=2, replica_groups=mesh['dp'=64,'proto'=4] {'dp'}, dimensions={0}, use_global_device_ids=true | all-gather | bytes 532480 | tf_op jit(solution)/shard_map/all_gather | solution.py:7
  109.4 0.1 reshape.28
  109.6 4.0 divide_reduce_fusion
  113.6 6.6 %psum.21 = f32[1024]{0:T(1024)S(1)} all-reduce(f32[1024]{0:T(1024)S(1)} %divide_reduce_fusion), channel_id=1, replica_groups=mesh['dp'=64,'proto'=4] {'proto'}, use_global_device_ids=true, to_apply=%region_4.0 | all-reduce | flops 1024 | bytes 8192 | tf_op jit(solution)/shard_map/psum | solution.py:21
  120.2 4.2 fusion.8
  124.3 51.0 %all-gather.1 = f32[131072]{0:T(1024)S(1)} all-gather(f32[2048]{0:T(1024)S(1)} %fusion.8), channel_id=3, replica_groups=mesh['dp'=64,'proto'=4] {'dp'}, dimensions={0}, use_global_device_ids=true | all-gather | bytes 532480 | tf_op jit(solution)/shard_map/all_gather | solution.py:7
  175.4 0.1 reshape.29
  175.5 4.4 fusion.10
  179.9 6.9 %psum.22 = f32[1024]{0:T(1024)S(1)} all-reduce(f32[1024]{0:T(1024)S(1)} %fusion.10), channel_id=1, replica_groups=mesh['dp'=64,'proto'=4] {'proto'}, use_global_device_ids=true, to_apply=%region_8.0 | all-reduce | flops 1024 | bytes 8192 | tf_op jit(solution)/shard_map/psum | solution.py:21
  186.8 0.0 copy-start
  186.8 4.6 fusion.11
  191.5 50.5 %all-gather.2 = f32[131072]{0:T(1024)S(1)} all-gather(f32[2048]{0:T(1024)S(1)} %fusion.11), channel_id=4, replica_groups=mesh['dp'=64,'proto'=4] {'dp'}, dimensions={0}, use_global_device_ids=true | all-gather | bytes 532480 | tf_op jit(solution)/shard_map/all_gather | solution.py:7
  242.0 0.1 reshape.30
  242.1 4.7 fusion.12
  246.8 6.6 %psum.23 = f32[1024]{0:T(1024)S(1)} all-reduce(f32[1024]{0:T(1024)S(1)} %fusion.12), channel_id=1, replica_groups=mesh['dp'=64,'proto'=4] {'proto'}, use_global_device_ids=true, to_apply=%region_12.0 | all-reduce | flops 1024 | bytes 8192 | tf_op jit(solution)/shard_map/psum | solution.py:21
  253.4 0.0 copy-done
  253.4 12.5 %fusion.13 = f32[2048,1024]{1,0:T(8,128)} fusion(bf16[1024,1024]{1,0:T(8,128)(2,1)S(1)} %copy-done, f32[1024,2048]{1,0:T(8,128)} %get-tuple-element.6, f32[1024]{0:T(1024)S(1)} %broadcast_multiply_fusion.3, f32[2048]{0:T(1024)S(1)} %broadcast_multiply_fusion, f32[1024]{0:T(1024)S(1)} %broadcast_multiply_fusion.4, f32[2048]{0:T(1024)S(1)} %broadcast_multiply_fusion.1, ...), kind=kOutput, calls=%fused_computation.17 | convolution fusion | flops 4311744512 | bytes 18911232 | tf_op jit(solution)/shard_map/dot_general | solution.py:40
  265.8 0.0 reduce-scatter.2.cloned.1.call-update
  265.9 0.0 all-gather.8.cloned.1.call-start
  265.9 145.7 %reduce-scatter.2.cloned.1.call-done = f32[32,1024]{1,0:T(8,128)} async-done(((f32[2048,1024]{1,0:T(8,128)}), f32[32,1024]{1,0:T(8,128)}) %reduce-scatter.2.cloned.1.call-update) | async-done | bytes 131088 | tf_op jit(solution)/shard_map/reduce_scatter | solution.py:39
  411.6 1.0 multiply_reduce_fusion
  412.6 1.6 multiply_convert_fusion
  414.2 0.0 all-gather.8.cloned.1.call-update
  414.2 82.6 %all-gather.8.cloned.1.call-done = bf16[2048,1024]{1,0:T(8,128)(2,1)} async-done(((bf16[32,1024]{1,0:T(8,128)(2,1)}), bf16[2048,1024]{1,0:T(8,128)(2,1)}) %all-gather.8.cloned.1.call-update) | async-done | bytes 4194320 | tf_op jit(solution)/shard_map/all_gather | solution.py:46
  496.9 4.6 copy.4
  (11 shorter events, 0.2 us)
Async XLA Ops:
  6.5 40.4 %all-gather.6.cloned.1.call-start = ((), (), s32[]{:S(2)}) async-start(), calls=%async_computation.1 | async-start | bytes 2621440 | tf_op jit(solution)/shard_map/all_gather | solution.py:26
  9.8 401.8 %reduce-scatter.2.cloned.1.call-start = ((), (), s32[]{:S(2)}) async-start(), calls=%async_computation.2 | async-start | bytes 8519680 | tf_op jit(solution)/shard_map/reduce_scatter | solution.py:39
  186.8 66.6 %copy-start = (bf16[1024,1024]{1,0:T(8,128)(2,1)S(1)}, bf16[1024,1024]{1,0:T(8,128)(2,1)}, u32[]{:S(2)}) copy-start(bf16[1024,1024]{1,0:T(8,128)(2,1)} %all-gather.6.cloned.1.call-done) | copy-start | bytes 6291460
  265.9 231.0 %all-gather.8.cloned.1.call-start = ((), (), s32[]{:S(2)}) async-start(), calls=%async_computation.3 | async-start | bytes 4259840 | tf_op jit(solution)/shard_map/all_gather | solution.py:46
Sparse Core Ops, SparseCore 0:
  9.9 36.9 all-gather.5
  266.0 145.5 reduce-scatter.1
  414.4 82.4 all-gather.7
